TPU v7x, 32 devices: a whole 2x2x4 slice. The times are simulated.
32 devices in a mesh: px: 16 (over z, y, x), py: 2 (over core).
Axes of the slice: x: 2, y: 2, z: 4, core: 2. Of those that a mesh axis runs over, the one named last changes fastest.
Arguments:
- start_value: float32 [128, 256, 256], P(None, 'px', 'py'), may hold values from -6 to 6
- prior: float32 [128, 256, 256], P('px', None, 'py'), may hold values from -6 to 6
- reach: float32 [256, 256], P('px', 'py'), may hold values from -6 to 6
- avoid: float32 [256, 256], P('px', 'py'), may hold values from -3 to 0.5
Outputs:
- final_value: float32 [128, 256, 256], P(None, 'px', 'py')
All inputs are finite; a program needn't handle non-finite values.
Results may differ from a plain program's by a relative error of at most 0.00002.
Values sent between devices are 32-bit elements; how exact they have to be, the bound alone decides.
No kernel may reach another device: no remote copies, remote signals or barrier semaphores. Data moves between devices by JAX's collectives and lax.ppermute only.
A program may use at most 64 MiB of HBM per device.

v0:
```python
import math
import jax
import jax.numpy as jnp
from jax import lax
from jax.sharding import PartitionSpec as P

epsilon = 1e-06
spacing = 1.0 / 64.0
speed = 1.0
turn_rate = 2.0
courant = 0.5


def extended_2(block, sides, width):
    for axis, dim in sides:
        count = lax.axis_size(axis)
        forward = [(i, i + 1) for i in range(count - 1)]
        backward = [(target, source) for source, target in forward]
        low = lax.ppermute(
            lax.slice_in_dim(block, block.shape[dim] - width, None, axis=dim), axis, forward
        )
        high = lax.ppermute(lax.slice_in_dim(block, 0, width, axis=dim), axis, backward)
        block = jnp.concatenate([low, block, high], axis=dim)
    return block


def upwind_blend(first, second, third, fourth, fifth):
    stencil_one = first / 3.0 - 7.0 * second / 6.0 + 11.0 * third / 6.0
    stencil_two = -second / 6.0 + 5.0 * third / 6.0 + fourth / 3.0
    stencil_three = third / 3.0 + 5.0 * fourth / 6.0 - fifth / 6.0
    smooth_one = 13.0 / 12.0 * jnp.square(first - 2.0 * second + third) + 0.25 * jnp.square(
        first - 4.0 * second + 3.0 * third
    )
    smooth_two = 13.0 / 12.0 * jnp.square(second - 2.0 * third + fourth) + 0.25 * jnp.square(
        second - fourth
    )
    smooth_three = 13.0 / 12.0 * jnp.square(third - 2.0 * fourth + fifth) + 0.25 * jnp.square(
        3.0 * third - 4.0 * fourth + fifth
    )
    weight_one = 0.1 / jnp.square(epsilon + smooth_one)
    weight_two = 0.6 / jnp.square(epsilon + smooth_two)
    weight_three = 0.3 / jnp.square(epsilon + smooth_three)
    total = weight_one * stencil_one + weight_two * stencil_two + weight_three * stencil_three
    return total / (weight_one + weight_two + weight_three)


def one_sided(padded, along, length, width):
    slopes = (
        lax.slice_in_dim(padded, 1, length + 6, axis=along)
        - lax.slice_in_dim(padded, 0, length + 5, axis=along)
    ) / width
    pieces = [lax.slice_in_dim(slopes, offset, offset + length, axis=along) for offset in range(6)]
    backward = upwind_blend(pieces[0], pieces[1], pieces[2], pieces[3], pieces[4])
    forward = upwind_blend(pieces[5], pieces[4], pieces[3], pieces[2], pieces[1])
    return (backward, forward)


def change_rate(extended):
    headings = extended.shape[0]
    row_count = extended.shape[1] - 6
    col_count = extended.shape[2] - 6
    heading_gap = 2.0 * math.pi / headings
    center = extended[:, 3 : 3 + row_count, 3 : 3 + col_count]
    west_slope, east_slope = one_sided(extended[:, :, 3 : 3 + col_count], 1, row_count, spacing)
    south_slope, north_slope = one_sided(extended[:, 3 : 3 + row_count, :], 2, col_count, spacing)
    wrapped = jnp.concatenate([center[headings - 3 :], center, center[:3]], axis=0)
    right_slope, left_slope = one_sided(wrapped, 0, headings, heading_gap)
    angles = heading_gap * jnp.arange(headings, dtype=jnp.float32)
    cosine = jnp.cos(angles)[:, None, None]
    sine_value = jnp.sin(angles)[:, None, None]
    result = cosine * speed * 0.5 * (west_slope + east_slope) + sine_value * speed * 0.5 * (
        south_slope + north_slope
    )
    result = result - turn_rate * jnp.abs(0.5 * (right_slope + left_slope))
    result = result + speed * jnp.abs(cosine) * 0.5 * (east_slope - west_slope)
    result = result + speed * jnp.abs(sine_value) * 0.5 * (north_slope - south_slope)
    return result + turn_rate * 0.5 * (left_slope - right_slope)


def section_update(extended):
    headings = extended.shape[0]
    heading_gap = 2.0 * math.pi / headings
    time_step = courant / (2.0 * speed / spacing + turn_rate / heading_gap)
    center = extended[:, 3 : extended.shape[1] - 3, 3 : extended.shape[2] - 3]
    return center + time_step * change_rate(extended)


def trim(field, margin):
    return field[:, margin : field.shape[1] - margin, margin : field.shape[2] - margin]


def on_device(start_value, prior, reach, avoid):
    regrouped = lax.all_to_all(prior, "px", split_axis=1, concat_axis=0, tiled=True)
    tile_rows = start_value.shape[1]
    tile_cols = start_value.shape[2]
    values = start_value
    row_pos = lax.axis_index("px") * tile_rows - 9 + jnp.arange(tile_rows + 18, dtype=jnp.int32)
    col_pos = lax.axis_index("py") * tile_cols - 9 + jnp.arange(tile_cols + 18, dtype=jnp.int32)
    row_inside = (row_pos >= 0) & (row_pos < tile_rows * lax.axis_size("px"))
    col_inside = (col_pos >= 0) & (col_pos < tile_cols * lax.axis_size("py"))
    inside = (row_inside[:, None] & col_inside[None, :]).astype(jnp.float32)[None]
    extended = extended_2(values, (("px", 1), ("py", 2)), 9)
    first = section_update(extended) * trim(inside, 3)
    second = (0.75 * trim(extended, 6) + 0.25 * section_update(first)) * trim(inside, 6)
    third = trim(extended, 9) / 3.0 + 2.0 / 3.0 * section_update(second)
    values = jnp.minimum(regrouped, jnp.maximum(avoid[None], jnp.minimum(reach[None], third)))
    return values


def solution(mesh):
    return jax.shard_map(
        on_device,
        mesh=mesh,
        in_specs=(P(None, "px", "py"), P("px", None, "py"), P("px", "py"), P("px", "py")),
        out_specs=P(None, "px", "py"),
        check_vma=False,
    )
```

profile of v0, /device:TPU:19, one launch (start us, length us, event | category | flops | bytes accessed | tf_op | source)
XLA Modules:
  0.0 142.8 jit_solution(3829122154147356272)
XLA Ops:
  0.0 1.7 %fusion.18 = (f32[128,9,128]{2,1,0:T(8,128)S(1)}, f32[128,9,128]{2,1,0:T(8,128)S(1)}) fusion(f32[128,16,128]{2,1,0:T(8,128)} %param.4), kind=kLoop, calls=%fused_computation.45 | loop fusion | bytes 2359296 | tf_op jit(solution)/shard_map/slice | solution.py:20
  1.7 0.0 copy-start.2
  1.7 0.2 copy.53
  1.9 3.3 %collective-permute-start = (f32[128,9,128]{2,0,1:T(8,128)S(1)}, f32[128,9,128]{2,0,1:T(8,128)}, u32[]{:S(2)}, u32[]{:S(2)}) collective-permute-start(f32[128,9,128]{2,0,1:T(8,128)S(1)} %copy.53), channel_id=1, source_target_pairs={{0,2},{2,4},{4,6},{6,8},{8,10},{10,12},{12,14},{14,16},{16,18},{18... | collective-permute-start | bytes 1769480 | tf_op jit(solution)/shard_map/ppermute | solution.py:19
  5.2 0.2 copy.54
  5.4 0.0 copy-start.1
  5.4 2.3 %collective-permute-start.1 = (f32[128,9,128]{2,0,1:T(8,128)S(1)}, f32[128,9,128]{2,0,1:T(8,128)}, u32[]{:S(2)}, u32[]{:S(2)}) collective-permute-start(f32[128,9,128]{2,0,1:T(8,128)S(1)} %copy.54), channel_id=1, source_target_pairs={{2,0},{4,2},{6,4},{8,6},{10,8},{12,10},{14,12},{16,14},{18,16},{20... | collective-permute-start | bytes 1769480 | tf_op jit(solution)/shard_map/ppermute | solution.py:22
  7.7 1.6 %copy.37 = f32[8,256,128]{2,0,1:T(8,128)} copy(f32[8,256,128]{2,1,0:T(8,128)S(1)} %copy-done.2) | data formatting | bytes 2097152 | tf_op args[1]
  9.3 7.3 %all-to-all-start = ((f32[8,256,128]{2,0,1:T(8,128)}), f32[8,256,128]{2,0,1:T(8,128)}, u32[]{:S(2)}, u32[]{:S(2)}) async-start(f32[8,256,128]{2,0,1:T(8,128)} %copy.37), calls=%async_computation | async-start | bytes 2097152 | tf_op jit(solution)/shard_map/all_to_all | solution.py:93
  16.6 0.4 copy.40
  17.1 0.1 and_convert_fusion
  17.2 0.1 slice_bitcast_fusion.1
  17.3 0.1 slice_bitcast_fusion
  17.3 16.9 %collective-permute-done = f32[128,9,128]{2,0,1:T(8,128)} collective-permute-done((f32[128,9,128]{2,0,1:T(8,128)S(1)}, f32[128,9,128]{2,0,1:T(8,128)}, u32[]{:S(2)}, u32[]{:S(2)}) %collective-permute-start) | collective-permute-done | bytes 589856 | tf_op jit(solution)/shard_map/ppermute | solution.py:19
  34.3 1.3 copy.43
  35.6 8.1 %collective-permute-done.1 = f32[128,9,128]{2,0,1:T(8,128)} collective-permute-done((f32[128,9,128]{2,0,1:T(8,128)S(1)}, f32[128,9,128]{2,0,1:T(8,128)}, u32[]{:S(2)}, u32[]{:S(2)}) %collective-permute-start.1) | collective-permute-done | bytes 589856 | tf_op jit(solution)/shard_map/ppermute | solution.py:22
  43.7 1.3 copy.45
  45.0 0.1 copy.46
  45.1 1.3 collective-permute-start.2
  46.4 0.1 copy.47
  46.4 4.2 %collective-permute-start.3 = (f32[128,34,9]{0,1,2:T(8,128)S(1)}, f32[128,34,9]{0,1,2:T(8,128)S(1)}, u32[]{:S(2)}, u32[]{:S(2)}) collective-permute-start(f32[128,34,9]{0,1,2:T(8,128)S(1)} %copy.47), channel_id=1, source_target_pairs={{1,0},{3,2},{5,4},{7,6},{9,8},{11,10},{13,12},{15,14},{17,16},{19,... | collective-permute-start | bytes 470024 | tf_op jit(solution)/shard_map/ppermute | solution.py:22
  50.7 0.0 collective-permute-done.2
  50.8 0.9 collective-permute-done.3
  51.7 0.2 pad_maximum_fusion.2
  52.0 0.7 fusion.15
  52.7 0.1 slice.380
  52.8 0.3 fusion.2
  53.1 0.3 fusion.3
  53.4 1.7 %pad_maximum_fusion = f32[134,28,140]{0,2,1:T(8,128)S(1)} fusion(f32[3,28,140]{0,2,1:T(8,128)S(1)} %get-tuple-element.6, f32[128,28,140]{0,2,1:T(8,128)S(1)} %slice.380, f32[3,28,140]{0,2,1:T(8,128)S(1)} %get-tuple-element.5), kind=kLoop, calls=%fused_computation.2 | loop fusion | flops 1050560 | bytes 4202240 | tf_op jit(solution)/shard_map/concatenate | solution.py:66
  55.1 1.1 fusion
  56.2 29.6 %add_multiply_fusion = f32[128,28,140]{0,2,1:T(8,128)S(1)} fusion(f32[133,28,140]{0,2,1:T(8,128)S(1)} %fusion, f32[128,28,145]{0,2,1:T(8,128)S(1)} %fusion.3, f32[128,33,140]{0,2,1:T(8,128)S(1)} %fusion.2, f32[28,140]{1,0:T(8,128)S(1)} %slice_bitcast_fusion, f32[128]{0:T(128)S(1)} %get-tuple-element.15, f32[128]{0:T(128)S(1)} %get-tuple-element.16, ...), kind=kLoop, calls=%fused_computation.14 | loop fusion | flops 197191680 | bytes 40158528 | tf_op jit(solution)/shard_map/mul | solution.py:103
  85.8 0.5 fusion.16
  86.4 0.1 slice.408
  86.5 0.3 fusion.5
  86.7 0.2 fusion.6
  86.9 1.3 pad_maximum_fusion.1
  88.2 0.9 fusion.1
  89.1 22.1 %fusion.8 = f32[128,22,134]{0,2,1:T(8,128)S(1)} fusion(f32[128,34,146]{0,2,1:T(8,128)S(1)} %pad_maximum_fusion.2, f32[133,22,134]{0,2,1:T(8,128)S(1)} %fusion.1, f32[128,22,139]{0,2,1:T(8,128)S(1)} %fusion.6, f32[128,27,134]{0,2,1:T(8,128)S(1)} %fusion.5, f32[22,134]{1,0:T(8,128)S(1)} %slice_bitcast_fusion.1, f32[128]{0:T(128)S(1)} %get-tuple-element.15, ...), kind=kLoop, calls=%fused_computation.21 | loop fusion | flops 149428224 | bytes 31710736 | tf_op jit(solution)/shard_map/mul | solution.py:104
  111.2 0.1 slice.436
  111.3 0.4 fusion.17
  111.7 0.9 pad_maximum_fusion.3
  112.6 0.1 fusion.10
  112.7 1.3 fusion.9
  114.0 2.0 %fusion.4 = f32[133,16,128]{0,2,1:T(8,128)} fusion(f32[134,16,128]{0,2,1:T(8,128)S(1)} %pad_maximum_fusion.3), kind=kLoop, calls=%fused_computation.12 | loop fusion | flops 544768 | bytes 3268608 | tf_op jit(solution)/shard_map/div | solution.py:48
  116.0 2.4 %copy.39 = f32[16,8,16,128]{3,2,1,0:T(8,128)} copy(f32[16,8,16,128]{3,1,2,0:T(8,128)} %bitcast.2) | data formatting | bytes 2097152 | tf_op jit(solution)/shard_map/all_to_all | solution.py:93
  118.4 2.6 %copy.50 = f32[128,16,128]{0,2,1:T(8,128)} copy(f32[128,16,128]{2,1,0:T(8,128)} %bitcast.8) | data formatting | bytes 2097152 | tf_op jit(solution)/shard_map/all_to_all | solution.py:93
  121.0 19.2 %maximum_minimum_fusion = f32[128,16,128]{0,2,1:T(8,128)} fusion(f32[128,16,128]{0,2,1:T(8,128)} %copy.50, f32[133,16,128]{0,2,1:T(8,128)} %fusion.4, f32[128,16,133]{0,2,1:T(8,128)S(1)} %fusion.10, f32[128,21,128]{0,2,1:T(8,128)} %fusion.9, f32[128,16,128]{0,2,1:T(8,128)} %copy-done, f32[128]{0:T(128)S(1)} %get-tuple-element.15, ...), kind=kLoop, calls=%fused_computation.26 | loop fusion | flops 104333312 | bytes 23087104 | tf_op jit(solution)/shard_map/min | solution.py:106
  140.2 2.6 %copy.51 = f32[128,16,128]{2,1,0:T(8,128)} copy(f32[128,16,128]{0,2,1:T(8,128)} %maximum_minimum_fusion) | data formatting | bytes 2097152 | tf_op jit(solution)/shard_map/min | solution.py:106
  (16 shorter events, 0.3 us)
Async XLA Ops:
  1.7 6.0 %copy-start.2 = (f32[8,256,128]{2,1,0:T(8,128)S(1)}, f32[8,256,128]{2,1,0:T(8,128)}, u32[]{:S(2)}) copy-start(f32[8,256,128]{2,1,0:T(8,128)} %param.5) | copy-start | bytes 3145732
  1.9 32.4 %collective-permute-start = (f32[128,9,128]{2,0,1:T(8,128)S(1)}, f32[128,9,128]{2,0,1:T(8,128)}, u32[]{:S(2)}, u32[]{:S(2)}) collective-permute-start(f32[128,9,128]{2,0,1:T(8,128)S(1)} %copy.53), channel_id=1, source_target_pairs={{0,2},{2,4},{4,6},{6,8},{8,10},{10,12},{12,14},{14,16},{16,18},{18... | collective-permute-start | bytes 1769480 | tf_op jit(solution)/shard_map/ppermute | solution.py:19
  5.4 11.2 %copy-start.1 = (f32[128,16,128]{2,1,0:T(8,128)S(1)}, f32[128,16,128]{2,1,0:T(8,128)}, u32[]{:S(2)}) copy-start(f32[128,16,128]{2,1,0:T(8,128)} %param.4) | copy-start | bytes 3145732
  5.4 38.3 %collective-permute-start.1 = (f32[128,9,128]{2,0,1:T(8,128)S(1)}, f32[128,9,128]{2,0,1:T(8,128)}, u32[]{:S(2)}, u32[]{:S(2)}) collective-permute-start(f32[128,9,128]{2,0,1:T(8,128)S(1)} %copy.54), channel_id=1, source_target_pairs={{2,0},{4,2},{6,4},{8,6},{10,8},{12,10},{14,12},{16,14},{18,16},{20... | collective-permute-start | bytes 1769480 | tf_op jit(solution)/shard_map/ppermute | solution.py:22
  9.3 106.7 %all-to-all-start = ((f32[8,256,128]{2,0,1:T(8,128)}), f32[8,256,128]{2,0,1:T(8,128)}, u32[]{:S(2)}, u32[]{:S(2)}) async-start(f32[8,256,128]{2,0,1:T(8,128)} %copy.37), calls=%async_computation | async-start | bytes 2097152 | tf_op jit(solution)/shard_map/all_to_all | solution.py:93
  17.1 34.6 %copy-start = (f32[128,16,128]{0,2,1:T(8,128)}, f32[128,16,128]{0,2,1:T(8,128)S(1)}, u32[]{:S(2)}) copy-start(f32[128,16,128]{0,2,1:T(8,128)S(1)} %copy.40) | copy-start | bytes 3145732
  45.1 5.6 %collective-permute-start.2 = (f32[128,34,9]{0,1,2:T(8,128)S(1)}, f32[128,34,9]{0,1,2:T(8,128)S(1)}, u32[]{:S(2)}, u32[]{:S(2)}) collective-permute-start(f32[128,34,9]{0,1,2:T(8,128)S(1)} %copy.46), channel_id=1, source_target_pairs={{0,1},{2,3},{4,5},{6,7},{8,9},{10,11},{12,13},{14,15},{16,17},{18,... | collective-permute-start | bytes 470024 | tf_op jit(solution)/shard_map/ppermute | solution.py:19
  46.4 5.2 %collective-permute-start.3 = (f32[128,34,9]{0,1,2:T(8,128)S(1)}, f32[128,34,9]{0,1,2:T(8,128)S(1)}, u32[]{:S(2)}, u32[]{:S(2)}) collective-permute-start(f32[128,34,9]{0,1,2:T(8,128)S(1)} %copy.47), channel_id=1, source_target_pairs={{1,0},{3,2},{5,4},{7,6},{9,8},{11,10},{13,12},{15,14},{17,16},{19,... | collective-permute-start | bytes 470024 | tf_op jit(solution)/shard_map/ppermute | solution.py:22
  116.0 5.0 %copy-start.3 = (f32[16,128]{1,0:T(8,128)S(1)}, f32[16,128]{1,0:T(8,128)}, u32[]{:S(2)}) copy-start(f32[16,128]{1,0:T(8,128)} %param.6) | copy-start | bytes 24580
  116.0 5.0 %copy-start.4 = (f32[16,128]{1,0:T(8,128)S(1)}, f32[16,128]{1,0:T(8,128)}, u32[]{:S(2)}) copy-start(f32[16,128]{1,0:T(8,128)} %param.7) | copy-start | bytes 24580
where the time goes:
time: 143 us
  other arithmetic  81.6 us (57%)
  waiting for transfers between devices  25.9 us (18%)
  starting transfers between devices  18.4 us (13%)
  local copies, waits for them, and re-layouts  16.6 us (12%)
    mul x1, other arithmetic, on_device(): first = section_update(extended) * trim(inside, 3)  29.6 us
    mul x1, other arithmetic, on_device(): (0.75 * trim(extended, 6) + 0.25 * section_update(first)) * trim(inside, 6)  22.1 us
    min x1, other arithmetic, on_device(): jnp.minimum(regrouped, jnp.maximum(avoid[None], jnp.minimum(reach[None],...  19.2 us
    ppermute x2, waiting for transfers between devices, extended_2(): lax.ppermute(lax.slice_in_dim(block, block.shape[dim] - width, None, axis...  16.9 us
    ppermute x2, waiting for transfers between devices, extended_2(): lax.ppermute(lax.slice_in_dim(block, 0, width, axis=dim), axis, backward)  8.95 us
    all_to_all x1, starting transfers between devices, on_device(): lax.all_to_all(prior, 'px', split_axis=1, concat_axis=0, tiled=True)  7.34 us
    ppermute x2, starting transfers between devices, extended_2(): lax.ppermute(lax.slice_in_dim(block, 0, width, axis=dim), axis, backward)  6.47 us
    div x9, other arithmetic, one_sided(): (lax.slice_in_dim(padded, 1, length + 6, axis=along) - lax.slice_in_dim(p...  6.45 us
  transfers between devices with their start and end apart: 5, of which 3 were waited for; matrix products, arithmetic and copies ran while one was open for 49% of the time, Pallas kernels for 0%

commit v1 on v0

--- a/solution.py
+++ b/solution.py
@@ -90,7 +90,10 @@
 
 
 def on_device(start_value, prior, reach, avoid):
-    regrouped = lax.all_to_all(prior, "px", split_axis=1, concat_axis=0, tiled=True)
+    arr_out = lax.all_to_all(
+        jnp.stack(jnp.split(prior, lax.psum(1, "px"), axis=1), axis=0), "px", 0, 0
+    )
+    regrouped = jnp.concatenate(arr_out, axis=0)
     tile_rows = start_value.shape[1]
     tile_cols = start_value.shape[2]
     values = start_value

time: 143 us -> 136 us (0.951)
  the two profiles are of different devices: /device:TPU:19 before, /device:TPU:3 now
where the time goes in v1:
time: 136 us
  other arithmetic  81.6 us (60%)
  starting transfers between devices  23 us (17%)
  local copies, waits for them, and re-layouts  22.7 us (17%)
  waiting for transfers between devices  7.89 us (6%)
    mul x1, other arithmetic, on_device(): first = section_update(extended) * trim(inside, 3)  29.6 us
    mul x1, other arithmetic, on_device(): (0.75 * trim(extended, 6) + 0.25 * section_update(first)) * trim(inside, 6)  22.1 us
    min x1, other arithmetic, on_device(): jnp.minimum(regrouped, jnp.maximum(avoid[None], jnp.minimum(reach[None],...  19.2 us
    ppermute x2, starting transfers between devices, extended_2(): lax.ppermute(lax.slice_in_dim(block, 0, width, axis=dim), axis, backward)  11.7 us
    unnamed x28, local copies, waits for them, and re-layouts  10.3 us
    all_to_all x1, starting transfers between devices, on_device(): lax.all_to_all(jnp.stack(jnp.split(prior, lax.psum(1, 'px'), axis=1), axi...  6.75 us
    div x9, other arithmetic, one_sided(): (lax.slice_in_dim(padded, 1, length + 6, axis=along) - lax.slice_in_dim(p...  6.45 us
    ppermute x2, waiting for transfers between devices, extended_2(): lax.ppermute(lax.slice_in_dim(block, block.shape[dim] - width, None, axis...  4.92 us
  transfers between devices with their start and end apart: 5, of which 3 were waited for; matrix products, arithmetic and copies ran while one was open for 58% of the time, Pallas kernels for 0%

profile of v1, /device:TPU:3, one launch (start us, length us, event | category | flops | bytes accessed | tf_op | source)
XLA Modules:
  0.0 135.6 jit_solution(5579672382028182673)
XLA Ops:
  0.0 1.7 %fusion.18 = (f32[128,9,128]{2,1,0:T(8,128)S(1)}, f32[128,9,128]{2,1,0:T(8,128)S(1)}) fusion(f32[128,16,128]{2,1,0:T(8,128)} %param.4), kind=kLoop, calls=%fused_computation.61 | loop fusion | bytes 2359296 | tf_op jit(solution)/shard_map/slice | solution.py:20
  1.9 3.3 %collective-permute-start = (f32[128,9,128]{2,0,1:T(8,128)S(1)}, f32[128,9,128]{2,0,1:T(8,128)}, u32[]{:S(2)}, u32[]{:S(2)}) collective-permute-start(f32[128,9,128]{2,0,1:T(8,128)S(1)} %copy.35), channel_id=1, source_target_pairs={{0,2},{2,4},{4,6},{6,8},{8,10},{10,12},{12,14},{14,16},{16,18},{18... | collective-permute-start | bytes 1769480 | tf_op jit(solution)/shard_map/ppermute | solution.py:19
  5.4 3.0 %collective-permute-start.1 = (f32[128,9,128]{2,0,1:T(8,128)S(1)}, f32[128,9,128]{2,0,1:T(8,128)}, u32[]{:S(2)}, u32[]{:S(2)}) collective-permute-start(f32[128,9,128]{2,0,1:T(8,128)S(1)} %copy.36), channel_id=1, source_target_pairs={{2,0},{4,2},{6,4},{8,6},{10,8},{12,10},{14,12},{16,14},{18,16},{20... | collective-permute-start | bytes 1769480 | tf_op jit(solution)/shard_map/ppermute | solution.py:22
  8.4 0.6 bitcast_dynamic-update-slice_fusion.15
  9.0 0.6 bitcast_dynamic-update-slice_fusion.14
  9.7 0.6 bitcast_dynamic-update-slice_fusion.13
  10.3 0.6 bitcast_dynamic-update-slice_fusion.12
  10.9 0.6 bitcast_dynamic-update-slice_fusion.11
  11.6 0.6 bitcast_dynamic-update-slice_fusion.10
  12.2 0.6 bitcast_dynamic-update-slice_fusion.9
  12.8 0.6 bitcast_dynamic-update-slice_fusion.8
  13.5 0.6 bitcast_dynamic-update-slice_fusion.7
  14.1 0.6 bitcast_dynamic-update-slice_fusion.6
  14.7 0.6 bitcast_dynamic-update-slice_fusion.5
  15.4 0.6 bitcast_dynamic-update-slice_fusion.4
  16.0 0.6 bitcast_dynamic-update-slice_fusion.3
  16.6 0.6 bitcast_dynamic-update-slice_fusion.2
  17.3 0.6 bitcast_dynamic-update-slice_fusion.1
  17.9 0.6 bitcast_dynamic-update-slice_fusion
  18.5 6.8 %all-to-all-start = ((f32[16,8,16,128]{3,2,1,0:T(8,128)}), f32[16,8,16,128]{3,2,1,0:T(8,128)}, u32[]{:S(2)}, u32[]{:S(2)}) async-start(f32[16,8,16,128]{3,2,1,0:T(8,128)} %bitcast_dynamic-update-slice_fusion), calls=%async_computation | async-start | bytes 2097152 | tf_op jit(solution)/shard_map/all_to_all | solution.py:93
  25.3 0.4 copy.23
  26.0 4.9 %collective-permute-done = f32[128,9,128]{2,0,1:T(8,128)} collective-permute-done((f32[128,9,128]{2,0,1:T(8,128)S(1)}, f32[128,9,128]{2,0,1:T(8,128)}, u32[]{:S(2)}, u32[]{:S(2)}) %collective-permute-start) | collective-permute-done | bytes 589856 | tf_op jit(solution)/shard_map/ppermute | solution.py:19
  30.9 1.3 copy.26
  32.2 2.1 %collective-permute-done.1 = f32[128,9,128]{2,0,1:T(8,128)} collective-permute-done((f32[128,9,128]{2,0,1:T(8,128)S(1)}, f32[128,9,128]{2,0,1:T(8,128)}, u32[]{:S(2)}, u32[]{:S(2)}) %collective-permute-start.1) | collective-permute-done | bytes 589856 | tf_op jit(solution)/shard_map/ppermute | solution.py:22
  34.3 1.3 copy.28
  35.7 1.3 collective-permute-start.2
  37.1 8.8 %collective-permute-start.3 = (f32[128,34,9]{0,1,2:T(8,128)S(1)}, f32[128,34,9]{0,1,2:T(8,128)S(1)}, u32[]{:S(2)}, u32[]{:S(2)}) collective-permute-start(f32[128,34,9]{0,1,2:T(8,128)S(1)} %copy.30), channel_id=1, source_target_pairs={{1,0},{3,2},{5,4},{7,6},{9,8},{11,10},{13,12},{15,14},{17,16},{19,... | collective-permute-start | bytes 470024 | tf_op jit(solution)/shard_map/ppermute | solution.py:22
  46.0 0.9 collective-permute-done.3
  46.9 0.2 pad_maximum_fusion.2
  47.2 0.7 fusion.15
  48.0 0.3 fusion.2
  48.4 0.3 fusion.3
  48.6 1.7 %pad_maximum_fusion = f32[134,28,140]{0,2,1:T(8,128)S(1)} fusion(f32[3,28,140]{0,2,1:T(8,128)S(1)} %get-tuple-element.6, f32[128,28,140]{0,2,1:T(8,128)S(1)} %slice.380, f32[3,28,140]{0,2,1:T(8,128)S(1)} %get-tuple-element.5), kind=kLoop, calls=%fused_computation.2 | loop fusion | flops 1050560 | bytes 4202240 | tf_op jit(solution)/shard_map/concatenate | solution.py:66
  50.3 1.1 fusion
  51.4 29.6 %add_multiply_fusion = f32[128,28,140]{0,2,1:T(8,128)S(1)} fusion(f32[133,28,140]{0,2,1:T(8,128)S(1)} %fusion, f32[128,28,145]{0,2,1:T(8,128)S(1)} %fusion.3, f32[128,33,140]{0,2,1:T(8,128)S(1)} %fusion.2, f32[28,140]{1,0:T(8,128)S(1)} %slice_bitcast_fusion, f32[128]{0:T(128)S(1)} %get-tuple-element.15, f32[128]{0:T(128)S(1)} %get-tuple-element.16, ...), kind=kLoop, calls=%fused_computation.14 | loop fusion | flops 197191680 | bytes 40158528 | tf_op jit(solution)/shard_map/mul | solution.py:106
  81.1 0.5 fusion.16
  81.7 0.3 fusion.5
  82.0 0.2 fusion.6
  82.2 1.3 pad_maximum_fusion.1
  83.4 0.9 fusion.1
  84.3 22.1 %fusion.8 = f32[128,22,134]{0,2,1:T(8,128)S(1)} fusion(f32[128,34,146]{0,2,1:T(8,128)S(1)} %pad_maximum_fusion.2, f32[133,22,134]{0,2,1:T(8,128)S(1)} %fusion.1, f32[128,22,139]{0,2,1:T(8,128)S(1)} %fusion.6, f32[128,27,134]{0,2,1:T(8,128)S(1)} %fusion.5, f32[22,134]{1,0:T(8,128)S(1)} %slice_bitcast_fusion.1, f32[128]{0:T(128)S(1)} %get-tuple-element.15, ...), kind=kLoop, calls=%fused_computation.21 | loop fusion | flops 149428224 | bytes 31710736 | tf_op jit(solution)/shard_map/mul | solution.py:107
  106.5 0.4 fusion.17
  106.9 0.9 pad_maximum_fusion.3
  108.0 1.3 fusion.9
  109.3 2.0 %fusion.4 = f32[133,16,128]{0,2,1:T(8,128)} fusion(f32[134,16,128]{0,2,1:T(8,128)S(1)} %pad_maximum_fusion.3), kind=kLoop, calls=%fused_computation.12 | loop fusion | flops 544768 | bytes 3268608 | tf_op jit(solution)/shard_map/div | solution.py:48
  111.2 2.6 %copy.33 = f32[128,16,128]{0,2,1:T(8,128)} copy(f32[128,16,128]{2,1,0:T(8,128)} %bitcast.16) | data formatting | bytes 2097152 | tf_op jit(solution)/shard_map/reshape | solution.py:96
  113.8 19.2 %maximum_minimum_fusion = f32[128,16,128]{0,2,1:T(8,128)} fusion(f32[128,16,128]{0,2,1:T(8,128)} %copy.33, f32[133,16,128]{0,2,1:T(8,128)} %fusion.4, f32[128,16,133]{0,2,1:T(8,128)S(1)} %fusion.10, f32[128,21,128]{0,2,1:T(8,128)} %fusion.9, f32[128,16,128]{0,2,1:T(8,128)} %copy-done, f32[128]{0:T(128)S(1)} %get-tuple-element.15, ...), kind=kLoop, calls=%fused_computation.26 | loop fusion | flops 104333312 | bytes 23087104 | tf_op jit(solution)/shard_map/min | solution.py:109
  133.0 2.6 %copy.34 = f32[128,16,128]{2,1,0:T(8,128)} copy(f32[128,16,128]{0,2,1:T(8,128)} %maximum_minimum_fusion) | data formatting | bytes 2097152 | tf_op jit(solution)/shard_map/min | solution.py:109
  (30 shorter events, 1.5 us)
Async XLA Ops:
  1.7 6.7 %copy-start.2 = (f32[8,256,128]{2,1,0:T(8,128)S(1)}, f32[8,256,128]{2,1,0:T(8,128)}, u32[]{:S(2)}) copy-start(f32[8,256,128]{2,1,0:T(8,128)} %param.5) | copy-start | bytes 3145732
  1.9 29.0 %collective-permute-start = (f32[128,9,128]{2,0,1:T(8,128)S(1)}, f32[128,9,128]{2,0,1:T(8,128)}, u32[]{:S(2)}, u32[]{:S(2)}) collective-permute-start(f32[128,9,128]{2,0,1:T(8,128)S(1)} %copy.35), channel_id=1, source_target_pairs={{0,2},{2,4},{4,6},{6,8},{8,10},{10,12},{12,14},{14,16},{16,18},{18... | collective-permute-start | bytes 1769480 | tf_op jit(solution)/shard_map/ppermute | solution.py:19
  5.4 28.9 %collective-permute-start.1 = (f32[128,9,128]{2,0,1:T(8,128)S(1)}, f32[128,9,128]{2,0,1:T(8,128)}, u32[]{:S(2)}, u32[]{:S(2)}) collective-permute-start(f32[128,9,128]{2,0,1:T(8,128)S(1)} %copy.36), channel_id=1, source_target_pairs={{2,0},{4,2},{6,4},{8,6},{10,8},{12,10},{14,12},{16,14},{18,16},{20... | collective-permute-start | bytes 1769480 | tf_op jit(solution)/shard_map/ppermute | solution.py:22
  9.0 16.3 %copy-start.1 = (f32[128,16,128]{2,1,0:T(8,128)S(1)}, f32[128,16,128]{2,1,0:T(8,128)}, u32[]{:S(2)}) copy-start(f32[128,16,128]{2,1,0:T(8,128)} %param.4) | copy-start | bytes 3145732
  18.5 92.7 %all-to-all-start = ((f32[16,8,16,128]{3,2,1,0:T(8,128)}), f32[16,8,16,128]{3,2,1,0:T(8,128)}, u32[]{:S(2)}, u32[]{:S(2)}) async-start(f32[16,8,16,128]{3,2,1,0:T(8,128)} %bitcast_dynamic-update-slice_fusion), calls=%async_computation | async-start | bytes 2097152 | tf_op jit(solution)/shard_map/all_to_all | solution.py:93
  25.7 21.2 %copy-start = (f32[128,16,128]{0,2,1:T(8,128)}, f32[128,16,128]{0,2,1:T(8,128)S(1)}, u32[]{:S(2)}) copy-start(f32[128,16,128]{0,2,1:T(8,128)S(1)} %copy.23) | copy-start | bytes 3145732
  35.7 10.2 %collective-permute-start.2 = (f32[128,34,9]{0,1,2:T(8,128)S(1)}, f32[128,34,9]{0,1,2:T(8,128)S(1)}, u32[]{:S(2)}, u32[]{:S(2)}) collective-permute-start(f32[128,34,9]{0,1,2:T(8,128)S(1)} %copy.29), channel_id=1, source_target_pairs={{0,1},{2,3},{4,5},{6,7},{8,9},{10,11},{12,13},{14,15},{16,17},{18,... | collective-permute-start | bytes 470024 | tf_op jit(solution)/shard_map/ppermute | solution.py:19
  37.1 9.8 %collective-permute-start.3 = (f32[128,34,9]{0,1,2:T(8,128)S(1)}, f32[128,34,9]{0,1,2:T(8,128)S(1)}, u32[]{:S(2)}, u32[]{:S(2)}) collective-permute-start(f32[128,34,9]{0,1,2:T(8,128)S(1)} %copy.30), channel_id=1, source_target_pairs={{1,0},{3,2},{5,4},{7,6},{9,8},{11,10},{13,12},{15,14},{17,16},{19,... | collective-permute-start | bytes 470024 | tf_op jit(solution)/shard_map/ppermute | solution.py:22
  111.2 2.6 %copy-start.3 = (f32[16,128]{1,0:T(8,128)S(1)}, f32[16,128]{1,0:T(8,128)}, u32[]{:S(2)}) copy-start(f32[16,128]{1,0:T(8,128)} %param.6) | copy-start | bytes 24580
  111.2 2.6 %copy-start.4 = (f32[16,128]{1,0:T(8,128)S(1)}, f32[16,128]{1,0:T(8,128)}, u32[]{:S(2)}) copy-start(f32[16,128]{1,0:T(8,128)} %param.7) | copy-start | bytes 24580
